TPU v7x, 32 devices: a whole 2x2x4 slice. The times are simulated.
32 devices in a mesh: ctx: 8 (over y, x, core), exp: 4 (over z).
Axes of the slice: x: 2, y: 2, z: 4, core: 2. Of those that a mesh axis runs over, the one named last changes fastest.
Arguments:
- mixer_input: bfloat16 [8192, 4096], P('ctx', 'exp'), may hold values from -6 to 6
- scale_exponent: int32 [64, 64], P('ctx', 'exp'), may hold values from -1 to 1
- step_size: float32 [64, 8192], P('exp', 'ctx'), may hold values from 0.25 to 1
- decay_log: float32 [64, 8192], P('exp', 'ctx'), may hold values from -1.2 to 0
- state_input: bfloat16 [8192, 128], P('ctx'), may hold values from -6 to 6
- state_output: bfloat16 [8192, 128], P('ctx'), may hold values from -0.5 to 0.5
- skip_gain: float32 [64], P('exp'), may hold values from 0.5 to 1.5
- gate_input: bfloat16 [8192, 4096], P('ctx', 'exp'), may hold values from -6 to 6
- norm_gain: float32 [4096], P('exp'), may hold values from 0.25 to 1.75
- up_weight: bfloat16 [4096, 3072], P('ctx', 'exp'), may hold values from -0.09375 to 0.09375
- down_weight: bfloat16 [3072, 4096], P('exp', 'ctx'), may hold values from -0.15625 to 0.15625
- expert_slot: int32 [8192], P('ctx'), may hold values from 0 to 256, as said below
- gate_prob: float32 [8192], P('ctx'), may hold values from 0.2 to 1
Outputs:
- layer_out: bfloat16 [8192, 4096], P('ctx', 'exp')
Inputs may be any that keep to these rules, and one draw needn't show every extreme that they name: `expert_slot`: within each aligned block of 1024 tokens, the tokens routed to the expert carry the distinct slots 0 to k - 1 for some k of at most 256, and all other tokens carry 256; in some block k equals 256.
All inputs are finite; a program needn't handle non-finite values.
Results may differ from a plain program's by a relative error of at most 0.0085.
Values may be sent and summed in bfloat16 or wider, within the bound.
No kernel may reach another device: no remote copies, remote signals or barrier semaphores. Data moves between devices by JAX's collectives and lax.ppermute only.
A program may use at most 128 MiB of HBM per device.

v0:
```python
import jax
import jax.numpy as jnp
from jax import lax
from jax.sharding import PartitionSpec as P

P_SIZE = 64
BLK = 128
CAP = 256
highest = lax.Precision.HIGHEST


def local_scan(x_in, step_size, decay_log, b_rows, c_rows):
    length, head_count, head_width = x_in.shape
    blocks = length // BLK
    x_blocks = x_in.reshape(blocks, BLK, head_count, head_width)
    b_blocks = b_rows.reshape(blocks, BLK, b_rows.shape[1])
    c_blocks = c_rows.reshape(blocks, BLK, c_rows.shape[1])
    step_blocks = step_size.reshape(head_count, blocks, BLK)
    cumulative = jnp.cumsum(decay_log.reshape(head_count, blocks, BLK), axis=2)
    scores = jnp.einsum("bin,bjn->bij", c_blocks, b_blocks, precision=highest)
    causal = jnp.arange(BLK)[:, None] >= jnp.arange(BLK)[None, :]
    spread = jnp.where(causal, cumulative[:, :, :, None] - cumulative[:, :, None, :], -jnp.inf)
    mixing = jnp.exp(spread) * scores[None] * step_blocks[:, :, None, :]
    inner_part = jnp.einsum("hbij,bjhp->bihp", mixing, x_blocks, precision=highest)
    tail_decay = jnp.exp(cumulative[:, :, -1:] - cumulative) * step_blocks
    block_state = jnp.einsum(
        "hbj,bjn,bjhp->bhnp", tail_decay, b_blocks, x_blocks, precision=highest
    )
    totals = cumulative[:, :, -1]

    def carry_on(running, block_items):
        block_total, block_end = block_items
        return (jnp.exp(block_total)[:, None, None] * running + block_end, running)

    running, entering = lax.scan(
        carry_on, jnp.zeros(block_state.shape[1:], jnp.float32), (totals.T, block_state)
    )
    carried = jnp.einsum(
        "bin,hbi,bhnp->bihp", c_blocks, jnp.exp(cumulative), entering, precision=highest
    )
    offsets = jnp.cumsum(totals, axis=1) - totals
    growth = jnp.exp(offsets[:, :, None] + cumulative)
    return (inner_part + carried, running, jnp.sum(totals, axis=1), c_blocks, growth)


def body(
    mixer_input,
    scale_exponent,
    step_size,
    decay_log,
    state_input,
    state_output,
    skip_gain,
    gate_input,
    norm_gain,
    up_weight,
    down_weight,
    expert_slot,
    gate_prob,
):
    length = mixer_input.shape[0]
    head_count = skip_gain.shape[0]
    blocks = length // BLK
    factor = jnp.exp2(scale_exponent.astype(jnp.float32))
    x_in = (
        mixer_input.astype(jnp.float32).reshape(blocks, BLK, head_count, P_SIZE)
        * factor[:, None, :, None]
    ).reshape(length, head_count, P_SIZE)
    b_rows = state_input.astype(jnp.float32)
    c_rows = state_output.astype(jnp.float32)
    local_out, end_state, total_log, c_blocks, growth = local_scan(
        x_in, step_size, decay_log, b_rows, c_rows
    )
    log_totals = lax.all_gather(total_log[None, :], "ctx", axis=0, tiled=True)
    before = jnp.cumsum(log_totals, axis=0) - log_totals
    position = lax.axis_index("ctx")
    own_prior = lax.dynamic_index_in_dim(before, position, 0, keepdims=False)
    shard_piece = lax.all_gather(
        end_state[None].astype(jnp.bfloat16), "ctx", axis=0, tiled=True
    ).astype(jnp.float32)
    row_count = shard_piece.shape[0]
    row_ids = jnp.arange(row_count, dtype=jnp.int32)
    decay_gap = jnp.minimum(own_prior[None, :] - before - log_totals, 0.0)
    weight = jnp.where((row_ids < position)[:, None], jnp.exp(decay_gap), 0.0)
    start_state = jnp.zeros_like(end_state) + jnp.einsum(
        "kh,khnp->hnp", weight, shard_piece, precision=highest
    )
    handed = jnp.einsum("bin,hbi,hnp->bihp", c_blocks, growth, start_state, precision=highest)
    mixer_out = (local_out + handed).reshape(length, head_count, P_SIZE) + skip_gain[
        None, :, None
    ] * x_in
    gated_out = mixer_out * jax.nn.silu(
        gate_input.astype(jnp.float32).reshape(length, head_count, P_SIZE)
    )
    inverse_rms = lax.rsqrt(jnp.mean(gated_out * gated_out, axis=2, keepdims=True) + 1e-05)
    normed = (
        (gated_out * inverse_rms * norm_gain.reshape(head_count, P_SIZE))
        .reshape(length, head_count * P_SIZE)
        .astype(jnp.bfloat16)
    )
    places = jnp.arange(CAP, dtype=jnp.int32)[:, None] == expert_slot[None, :]
    picker = places.astype(jnp.bfloat16)
    dispatched = jnp.dot(picker, normed, preferred_element_type=jnp.float32).astype(jnp.bfloat16)
    full_features = lax.all_gather(dispatched, "exp", axis=1, tiled=True)
    up_act = jnp.dot(
        full_features,
        lax.all_gather(up_weight, "ctx", axis=0, tiled=True),
        preferred_element_type=jnp.float32,
    )
    hidden = jax.nn.silu(up_act).astype(jnp.bfloat16)
    terms = jnp.dot(
        hidden,
        lax.all_gather(down_weight, "ctx", axis=1, tiled=True),
        preferred_element_type=jnp.float32,
    )
    own_sums = lax.psum_scatter(
        terms.astype(jnp.bfloat16), "exp", scatter_dimension=1, tiled=True
    ).astype(jnp.float32)
    selector = places.astype(jnp.float32)
    expert_tok = lax.dot_general(selector, own_sums, (((0,), (0,)), ((), ())), precision=highest)
    return (normed.astype(jnp.float32) + gate_prob[:, None] * expert_tok).astype(jnp.bfloat16)


def solution(mesh):
    in_specs = (
        P("ctx", "exp"),
        P("ctx", "exp"),
        P("exp", "ctx"),
        P("exp", "ctx"),
        P("ctx", None),
        P("ctx", None),
        P("exp"),
        P("ctx", "exp"),
        P("exp"),
        P("ctx", "exp"),
        P("exp", "ctx"),
        P("ctx"),
        P("ctx"),
    )
    out_specs = P("ctx", "exp")
    return jax.shard_map(body, mesh=mesh, in_specs=in_specs, out_specs=out_specs, check_vma=False)
```

profile of v0, /device:TPU:0, one launch (start us, length us, event | category | flops | bytes accessed | tf_op | source)
XLA Modules:
  0.0 375.8 jit_solution(6003521538814983370)
XLA Ops:
  6.5 0.9 copy.117
  7.4 4.5 %reduce_window_sum.33 = f32[16,8,128]{2,1,0:T(8,128)S(1)} reduce-window(f32[16,8,128]{2,1,0:T(8,128)S(1)} %bitcast.107, f32[]{:T(128)} %constant.28.clone.1), window={size=1x1x128 pad=0_0x0_0x127_0}, to_apply=%region_0.0 | reduce-window | flops 2080768 | bytes 131076 | tf_op jit(solution)/shard_map/jit(cumsum)/reduce_window_sum | solution.py:19
  12.4 0.3 slice_reduce_fusion
  12.9 0.9 copy.118
  13.9 0.7 multiply_exponential_fusion
  14.6 6.8 %reshape.91 = f32[8,128,16,64]{3,2,1,0:T(8,128)} reshape(bf16[1024,1024]{1,0:T(8,128)(2,1)} %param.15) | data formatting | bytes 6291456 | tf_op jit(solution)/shard_map/reshape | solution.py:66
  21.4 7.2 %copy.74 = f32[8,128,16,64]{1,3,2,0:T(8,128)} copy(f32[8,128,16,64]{3,2,1,0:T(8,128)} %reshape.91) | data formatting | bytes 8388608 | tf_op jit(solution)/shard_map/reshape | solution.py:66
  28.5 6.4 %fusion.20 = f32[8,16,128,64]{2,3,1,0:T(8,128)} fusion(bf16[8,128,128,1]{2,1,3,0:T(8,128)(2,1)S(1)} %bitcast.102, f32[8,128,16,64]{1,3,2,0:T(8,128)} %copy.74, f32[8,128,16]{1,2,0:T(8,128)S(1)} %copy.81, f32[8,16]{1,0:T(8,128)S(1)} %multiply_exponential_fusion), kind=kOutput, calls=%fused_computation.31 | convolution fusion | flops 1612709888 | bytes 8716800 | tf_op jit(solution)/shard_map/hbj,bjn,bjhp->bhnp/dot_general | solution.py:26
  35.0 21.8 %while.13 = (s32[]{:T(128)}, f32[16,128,64]{2,1,0:T(8,128)S(1)}, f32[8,16,128,64]{3,2,1,0:T(8,128)}, f32[8,16]{1,0:T(8,128)S(1)}, f32[8,16,128,64]{2,3,1,0:T(8,128)}, /*index=5*/s32[]{:T(128)}, s32[]{:T(128)}) while((s32[]{:T(128)}, f32[16,128,64]{2,1,0:T(8,128)S(1)}, f32[8,16,128,64]{3,2,1,0:T(8,128)}, f32[8,16]{1,0:T(8,128)S(1)}, ...), condition=%wide.region_2.3_spmd.clone, body=%wide.region_1.2_spmd.clone.sunk | while | flops 524291 | bytes 5243680 | solution.py:35
  35.0 1.0 bitcast_dynamic-update-slice_fusion.2
  36.0 1.1 constant_dynamic-slice_fusion.3
  37.1 0.3 copy.125
  37.4 0.2 bitcast_add_fusion.2
  37.7 1.1 bitcast_dynamic-update-slice_fusion.2
  38.8 1.1 constant_dynamic-slice_fusion.3
  39.8 0.3 copy.125
  40.2 0.2 bitcast_add_fusion.2
  40.4 1.1 bitcast_dynamic-update-slice_fusion.2
  41.5 1.1 constant_dynamic-slice_fusion.3
  42.6 0.3 copy.125
  43.1 1.1 bitcast_dynamic-update-slice_fusion.2
  44.2 1.1 constant_dynamic-slice_fusion.3
  45.3 0.3 copy.125
  45.8 1.0 bitcast_dynamic-update-slice_fusion.2
  46.9 1.1 constant_dynamic-slice_fusion.3
  48.0 0.3 copy.125
  48.3 0.2 bitcast_add_fusion.2
  48.5 1.1 bitcast_dynamic-update-slice_fusion.2
  49.6 1.1 constant_dynamic-slice_fusion.3
  50.7 0.3 copy.125
  51.3 1.1 bitcast_dynamic-update-slice_fusion.2
  52.4 1.1 constant_dynamic-slice_fusion.3
  53.4 0.3 copy.125
  54.0 1.1 bitcast_dynamic-update-slice_fusion.2
  55.1 1.1 constant_dynamic-slice_fusion.3
  56.2 0.3 copy.125
  56.8 0.9 copy.87
  57.8 0.6 dynamic-slice
  59.1 0.2 dynamic-update-slice
  59.4 15.6 %all-reduce = f32[128]{0:T(128)S(1)} all-reduce(f32[128]{0:T(128)S(1)} %dynamic-update-slice), channel_id=2, replica_groups=mesh['ctx'=8,'exp'=4] {'ctx'}, use_global_device_ids=true, to_apply=%add | all-reduce | flops 128 | bytes 1024
  75.1 6.8 %reshape.93 = f32[8,128,16,64]{3,2,1,0:T(8,128)} reshape(bf16[1024,1024]{1,0:T(8,128)(2,1)} %param.22) | data formatting | bytes 6291456 | tf_op jit(solution)/shard_map/reshape | solution.py:93
  81.9 7.2 %copy.94 = f32[8,128,16,64]{1,3,2,0:T(8,128)} copy(f32[8,128,16,64]{3,2,1,0:T(8,128)} %reshape.93) | data formatting | bytes 8388608 | tf_op jit(solution)/shard_map/reshape | solution.py:93
  89.2 2.5 mul.135
  91.6 5.4 %copy.90 = f32[1024,1024]{1,0:T(8,128)} copy(f32[1024,1024]{0,1:T(8,128)} %bitcast.99) | data formatting | bytes 8388608 | tf_op jit(solution)/shard_map/mul | solution.py:66
  97.3 0.3 fusion.34
  97.6 12.1 %fusion.35 = f32[8,16,64,128]{3,2,1,0:T(8,128)} fusion(f32[8,16,128,64]{3,2,1,0:T(8,128)} %get-tuple-element.33, bf16[8,128,128,1]{2,1,3,0:T(8,128)(2,1)S(1)} %bitcast.96), kind=kOutput, calls=%fused_computation.60 | convolution fusion | flops 1610612736 | bytes 8650752 | tf_op jit(solution)/shard_map/bin,hbi,bhnp->bihp/dot_general | solution.py:38
  109.8 18.0 %fusion.2 = f32[8,16,64,128]{3,2,1,0:T(8,128)} fusion(f32[16,8,128]{2,0,1:T(8,128)S(1)} %copy_bitcast_fusion.2, f32[8,128,128]{2,1,0:T(8,128)S(1)} %fusion.34, f32[16,8,128]{2,0,1:T(8,128)S(1)} %copy.75, pred[128,128]{1,0:T(8,128)(4,1)S(1)} %iota_compare_fusion.3, f32[8,128,16,64]{1,3,2,0:T(8,128)S(1)} %copy-done.2, f32[8,16]{1,0:T(8,128)S(1)} %multiply_exponential_fusion), kind=kOutput, calls=%fused_computation.6 | convolution fusion | flops 1620049920 | bytes 9060864 | tf_op jit(solution)/shard_map/hbij,bjhp->bihp/dot_general | solution.py:24
  127.7 2.1 multiply_reduce_fusion
  129.8 9.3 %multiply_reduce_fusion.1 = (f32[8,128,16]{1,2,0:T(8,128)S(1)}, f32[8,128,16,64]{1,3,2,0:T(8,128)}) fusion(f32[8,128,16,64]{1,3,2,0:T(8,128)} %copy.94, f32[8,128,16,64]{1,3,2,0:T(8,128)} %copy.74, f32[16]{0:T(128)S(1)} %copy-done.9, f32[8,16]{1,0:T(8,128)S(1)} %multiply_exponential_fusion, bf16[8,128,128,1]{2,1,3,0:T(8,128)(2,1)S(1)} %bitcast.97, ...), kind=kOutput, calls=%fused_computation.20 | convolution fusion | flops 1625276416 | bytes 21955136 | tf_op jit(solution)/shard_map/bin,hbi,hnp->bihp/dot_general | solution.py:88
  139.1 7.1 %copy.110 = f32[8,128,16,64]{3,2,1,0:T(8,128)} copy(f32[8,128,16,64]{1,3,2,0:T(8,128)} %get-tuple-element.89) | data formatting | bytes 8388608 | tf_op jit(solution)/shard_map/reshape | solution.py:89
  146.3 7.6 %reshape.92 = f32[1024,1024]{1,0:T(8,128)} reshape(f32[8,128,16,64]{3,2,1,0:T(8,128)} %copy.110) | data formatting | bytes 8388608 | tf_op jit(solution)/shard_map/reshape | solution.py:89
  153.9 2.5 mul.146
  156.4 5.5 %copy.96 = f32[1024,1024]{1,0:T(8,128)} copy(f32[1024,1024]{0,1:T(8,128)} %bitcast.100) | data formatting | bytes 8388608 | tf_op jit(solution)/shard_map/mul | solution.py:97
  161.9 6.6 %multiply_convert_fusion = bf16[1024,1024]{1,0:T(8,128)(2,1)S(1)} fusion(f32[1024,1024]{1,0:T(8,128)} %copy.96, f32[1024,1024]{1,0:T(8,128)} %reshape.92, f32[1024,1024]{1,0:T(8,128)} %copy.90, f32[1024]{0:T(1024)S(1)} %copy-done.8, f32[1024]{0:T(1024)S(1)} %mul.131, bf16[1024,1024]{1,0:T(8,128)(2,1)S(1)} %copy-done.3, bf16[1024,1024]{1,0:T(8,128)(2,1)} %param.15), kind=kLoop, calls=%fused_computation.19 | loop fusion | flops 13631488 | bytes 18882560 | tf_op jit(solution)/shard_map/convert_element_type | solution.py:99
  168.5 1.3 copy-done.4
  169.9 1.5 convolution_convert_fusion.1
  171.5 0.7 all-gather.11.cloned.1.call-update
  172.2 0.5 all-gather.9.cloned.1.call-update
  172.8 43.8 %all-gather.7.cloned.1.call-done = bf16[256,4096]{1,0:T(8,128)(2,1)} async-done(((bf16[256,1024]{1,0:T(8,128)(2,1)}), bf16[256,4096]{1,0:T(8,128)(2,1)}) %all-gather.7.cloned.1.call-update) | async-done | bytes 2097168 | tf_op jit(solution)/shard_map/all_gather | solution.py:104
  216.6 47.3 %all-gather.11.cloned.1.call-done = bf16[768,4096]{1,0:T(8,128)(2,1)} async-done(((bf16[768,512]{1,0:T(8,128)(2,1)}), bf16[768,4096]{1,0:T(8,128)(2,1)}) %all-gather.11.cloned.1.call-update) | async-done | bytes 6291472 | tf_op jit(solution)/shard_map/all_gather | solution.py:113
  263.9 47.2 %all-gather.9.cloned.1.call-done = bf16[4096,768]{1,0:T(8,128)(2,1)} async-done(((bf16[512,768]{1,0:T(8,128)(2,1)}), bf16[4096,768]{1,0:T(8,128)(2,1)}) %all-gather.9.cloned.1.call-update) | async-done | bytes 6291472 | tf_op jit(solution)/shard_map/all_gather | solution.py:107
  311.1 11.1 %convolution_convert_fusion = bf16[256,4096]{1,0:T(8,128)(2,1)} fusion(bf16[768,4096]{1,0:T(8,128)(2,1)} %all-gather.11.cloned.1.call-done, bf16[256,4096]{1,0:T(8,128)(2,1)} %all-gather.7.cloned.1.call-done, bf16[4096,768]{1,0:T(8,128)(2,1)} %all-gather.9.cloned.1.call-done), kind=kOutput, calls=%fused_computation.12 | convolution fusion | flops 3223257088 | bytes 16777216 | tf_op jit(solution)/shard_map/dot_general | solution.py:111
  322.2 43.8 %reduce-scatter.2.cloned.1.call-done = bf16[256,1024]{1,0:T(8,128)(2,1)} async-done(((bf16[256,4096]{1,0:T(8,128)(2,1)}), bf16[256,1024]{1,0:T(8,128)(2,1)}) %reduce-scatter.2.cloned.1.call-update) | async-done | bytes 524304 | tf_op jit(solution)/shard_map/reduce_scatter | solution.py:116
  366.0 3.3 add_convert_fusion
  (74 shorter events, 2.6 us)
Async XLA Ops:
  6.5 90.8 %copy-start = (bf16[1024,128]{1,0:T(8,128)(2,1)S(1)}, bf16[1024,128]{1,0:T(8,128)(2,1)}, u32[]{:S(2)}) copy-start(bf16[1024,128]{1,0:T(8,128)(2,1)} %param.20) | copy-start | bytes 786436
  6.5 121.2 %all-gather.13.cloned.1.call-start = ((), (), s32[]{:S(2)}) async-start(), calls=%async_computation.5 | async-start | bytes 2359296 | tf_op jit(solution)/shard_map/all_gather | solution.py:78
  21.4 7.2 %copy-start.6 = (bf16[1024,128]{1,0:T(8,128)(2,1)S(1)}, bf16[1024,128]{1,0:T(8,128)(2,1)}, u32[]{:S(2)}) copy-start(bf16[1024,128]{1,0:T(8,128)(2,1)} %param.19) | copy-start | bytes 786436
  35.0 22.9 %copy-start.12 = (u32[32]{0:T(128)S(1)}, u32[32]{0:T(128)}, u32[]{:S(2)}) copy-start(u32[32]{0:T(128)} %constant.54) | copy-start | bytes 388
  57.7 158.9 %all-gather.7.cloned.1.call-start = ((), (), s32[]{:S(2)}) async-start(), calls=%async_computation.1 | async-start | bytes 2621440 | tf_op jit(solution)/shard_map/all_gather | solution.py:104
  91.6 5.4 %copy-start.9 = (f32[16]{0:T(128)S(1)}, f32[16]{0:T(128)}, u32[]{:S(2)}) copy-start(f32[16]{0:T(128)} %param.21) | copy-start | bytes 196
  91.6 5.7 %copy-start.7 = (f32[16,1024]{1,0:T(8,128)S(1)}, f32[16,1024]{1,0:T(8,128)}, u32[]{:S(2)}) copy-start(f32[16,1024]{1,0:T(8,128)} %param.17) | copy-start | bytes 196612
  97.6 12.1 %copy-start.2 = (f32[8,128,16,64]{1,3,2,0:T(8,128)S(1)}, f32[8,128,16,64]{1,3,2,0:T(8,128)}, u32[]{:S(2)}) copy-start(f32[8,128,16,64]{1,3,2,0:T(8,128)} %copy.74) | copy-start | bytes 12582916
  156.4 5.5 %copy-start.3 = (bf16[1024,1024]{1,0:T(8,128)(2,1)S(1)}, bf16[1024,1024]{1,0:T(8,128)(2,1)}, u32[]{:S(2)}) copy-start(bf16[1024,1024]{1,0:T(8,128)(2,1)} %param.22) | copy-start | bytes 6291460
  156.4 5.5 %copy-start.8 = (f32[1024]{0:T(1024)S(1)}, f32[1024]{0:T(1024)}, u32[]{:S(2)}) copy-start(f32[1024]{0:T(1024)} %param.23) | copy-start | bytes 12292
  161.9 7.9 %copy-start.10 = (s32[1024]{0:T(1024)S(1)}, s32[1024]{0:T(1024)}, u32[]{:S(2)}) copy-start(s32[1024]{0:T(1024)} %param.26) | copy-start | bytes 12292
  168.5 1.3 copy-start.4
  171.4 92.5 %all-gather.11.cloned.1.call-start = ((), (), s32[]{:S(2)}) async-start(), calls=%async_computation.3 | async-start | bytes 7077888 | tf_op jit(solution)/shard_map/all_gather | solution.py:113
  172.2 138.9 %all-gather.9.cloned.1.call-start = ((), (), s32[]{:S(2)}) async-start(), calls=%async_computation.2 | async-start | bytes 7077888 | tf_op jit(solution)/shard_map/all_gather | solution.py:107
  172.7 193.2 %copy-start.5 = (bf16[1024,1024]{1,0:T(8,128)(2,1)S(1)}, bf16[1024,1024]{1,0:T(8,128)(2,1)}, u32[]{:S(2)}) copy-start(bf16[1024,1024]{1,0:T(8,128)(2,1)} %copy-done.4) | copy-start | bytes 6291460
  172.8 193.2 %copy-start.11 = (f32[1024]{0:T(1024)S(1)}, f32[1024]{0:T(1024)}, u32[]{:S(2)}) copy-start(f32[1024]{0:T(1024)} %param.27) | copy-start | bytes 12292
  172.8 193.2 %reduce-scatter.2.cloned.1.call-start = ((), (), s32[]{:S(2)}) async-start(), calls=%async_computation.4 | async-start | bytes 2621440 | tf_op jit(solution)/shard_map/reduce_scatter | solution.py:116
  311.1 58.2 %copy-start.1 = (bf16[1024,128]{1,0:T(8,128)(2,1)S(1)}, bf16[1024,128]{1,0:T(8,128)(2,1)}, u32[]{:S(2)}) copy-start(bf16[1024,128]{1,0:T(8,128)(2,1)} %param.20) | copy-start | bytes 786436
Sparse Core Ops, SparseCore 0:
  57.8 30.5 all-gather.12
  171.5 45.0 all-gather.6
  218.5 45.3 all-gather.10
  265.6 45.3 all-gather.8
  322.3 43.6 reduce-scatter.1
where the time goes:
time: 377 us; the launch traced here: 376 us
  waiting for transfers between devices  183 us (49%)
  local copies, waits for them, and re-layouts  75.8 us (20%)
  matrix products  62 us (16%)
  other arithmetic  24.6 us (7%)
  blocking collectives  15.6 us (4%)
  between operations  14 us (4%)
    all_gather x1, waiting for transfers between devices, body(): lax.all_gather(down_weight, 'ctx', axis=1, tiled=True)  47.3 us
    all_gather x1, waiting for transfers between devices, body(): lax.all_gather(up_weight, 'ctx', axis=0, tiled=True)  47.2 us
    all_gather x1, waiting for transfers between devices, body(): full_features = lax.all_gather(dispatched, 'exp', axis=1, tiled=True)  43.8 us
    reduce_scatter x1, waiting for transfers between devices, body(): lax.psum_scatter(terms.astype(jnp.bfloat16), 'exp', scatter_dimension=1,...  43.8 us
    dot_general x1, matrix products, local_scan(): jnp.einsum('hbij,bjhp->bihp', mixing, x_blocks, precision=highest)  18 us
    unnamed x1, blocking collectives  15.6 us
    reshape x2, local copies, waits for them, and re-layouts, body(): (local_out + handed).reshape(length, head_count, P_SIZE)  14.8 us
    reshape x2, local copies, waits for them, and re-layouts, body(): gate_input.astype(jnp.float32).reshape(length, head_count, P_SIZE)  14 us
  transfers between devices with their start and end apart: 5, of which 4 were waited for; matrix products, arithmetic and copies ran while one was open for 14% of the time, Pallas kernels for 0%

commit v1 on v0

--- a/solution.py
+++ b/solution.py
@@ -101,7 +101,12 @@
     places = jnp.arange(CAP, dtype=jnp.int32)[:, None] == expert_slot[None, :]
     picker = places.astype(jnp.bfloat16)
     dispatched = jnp.dot(picker, normed, preferred_element_type=jnp.float32).astype(jnp.bfloat16)
-    full_features = lax.all_gather(dispatched, "exp", axis=1, tiled=True)
+    ring = [dispatched]
+    for hop in range(3):
+        ring.append(lax.ppermute(ring[-1], "exp", [(dev, (dev + 1) % 4) for dev in range(4)]))
+    full_features = jnp.roll(
+        jnp.concatenate(ring[::-1], axis=1), (lax.axis_index("exp") + 1) * ring[0].shape[1], axis=1
+    )
     up_act = jnp.dot(
         full_features,
         lax.all_gather(up_weight, "ctx", axis=0, tiled=True),

time: 377 us -> 287 us (0.76)
  waiting for transfers between devices: 183 us -> 85.4 us
  local copies, waits for them, and re-layouts: 75.8 us -> 81.3 us
    all_gather x1, waiting for transfers between devices: 47.3 us -> 0.01 us  [body(): lax.all_gather(down_weight, 'ctx', axis=1, tiled=True)]
    all_gather x1, waiting for transfers between devices: 47.2 us -> 0.01 us  [body(): lax.all_gather(up_weight, 'ctx', axis=0, tiled=True)]
    all_gather x1 -> x0, waiting for transfers between devices: 43.8 us -> none  [body(): full_features = lax.all_gather(dispatched, 'exp', axis=1, tiled=True)]
    ppermute x0 -> x3, waiting for transfers between devices: none -> 39.4 us  [body(): lax.ppermute(ring[-1], 'exp', [(dev, (dev + 1) % 4) for dev in range(4)])]
    unnamed x32 -> x41, local copies, waits for them, and re-layouts: 4.04 us -> 10.1 us
  transfers between devices with their start and end apart: 5 -> 7, of which waited for: 4 -> 4; matrix products, arithmetic and copies ran while one was open for 14% -> 36% of each run, Pallas kernels for 0% -> 0%
where the time goes in v1:
time: 287 us; the launch traced here: 286 us
  waiting for transfers between devices  85.4 us (30%)
  local copies, waits for them, and re-layouts  81.3 us (28%)
  matrix products  61.9 us (22%)
  other arithmetic  25.5 us (9%)
  blocking collectives  15.5 us (5%)
  between operations  14 us (5%)
    reduce_scatter x1, waiting for transfers between devices, body(): lax.psum_scatter(terms.astype(jnp.bfloat16), 'exp', scatter_dimension=1,...  44.6 us
    ppermute x3, waiting for transfers between devices, body(): lax.ppermute(ring[-1], 'exp', [(dev, (dev + 1) % 4) for dev in range(4)])  39.4 us
    dot_general x1, matrix products, local_scan(): jnp.einsum('hbij,bjhp->bihp', mixing, x_blocks, precision=highest)  18 us
    unnamed x1, blocking collectives  15.5 us
    reshape x2, local copies, waits for them, and re-layouts, body(): (local_out + handed).reshape(length, head_count, P_SIZE)  14.9 us
    reshape x2, local copies, waits for them, and re-layouts, body(): mixer_input.astype(jnp.float32).reshape(blocks, BLK, head_count, P_SIZE)  14 us
    dot_general x1, matrix products, local_scan(): jnp.einsum('bin,hbi,bhnp->bihp', c_blocks, jnp.exp(cumulative), entering,...  12.5 us
    reshape x2, local copies, waits for them, and re-layouts, body(): gate_input.astype(jnp.float32).reshape(length, head_count, P_SIZE)  11.7 us
  transfers between devices with their start and end apart: 7, of which 4 were waited for; matrix products, arithmetic and copies ran while one was open for 36% of the time, Pallas kernels for 0%

profile of v1, /device:TPU:0, one launch (start us, length us, event | category | flops | bytes accessed | tf_op | source)
XLA Modules:
  0.0 285.8 jit_solution(8292433175519200548)
XLA Ops:
  6.5 0.9 copy.117
  7.4 4.5 %reduce_window_sum.33 = f32[16,8,128]{2,1,0:T(8,128)S(1)} reduce-window(f32[16,8,128]{2,1,0:T(8,128)S(1)} %bitcast.106, f32[]{:T(128)} %constant.65.clone.1), window={size=1x1x128 pad=0_0x0_0x127_0}, to_apply=%region_0.0 | reduce-window | flops 2080768 | bytes 131076 | tf_op jit(solution)/shard_map/jit(cumsum)/reduce_window_sum | solution.py:19
  12.9 0.9 copy.118
  13.7 0.6 exponential_bitcast_fusion.1
  14.4 0.7 multiply_exponential_fusion
  15.1 6.8 %reshape.91 = f32[8,128,16,64]{3,2,1,0:T(8,128)} reshape(bf16[1024,1024]{1,0:T(8,128)(2,1)} %param.15) | data formatting | bytes 6291456 | tf_op jit(solution)/shard_map/reshape | solution.py:66
  21.9 7.1 %copy.74 = f32[8,128,16,64]{1,3,2,0:T(8,128)} copy(f32[8,128,16,64]{3,2,1,0:T(8,128)} %reshape.91) | data formatting | bytes 8388608 | tf_op jit(solution)/shard_map/reshape | solution.py:66
  29.1 6.4 %fusion.20 = f32[8,16,128,64]{2,3,1,0:T(8,128)} fusion(bf16[8,128,128,1]{2,1,3,0:T(8,128)(2,1)S(1)} %bitcast.101, f32[8,128,16,64]{1,3,2,0:T(8,128)} %copy.74, f32[8,128,16]{1,2,0:T(8,128)S(1)} %copy.81, f32[8,16]{1,0:T(8,128)S(1)} %multiply_exponential_fusion), kind=kOutput, calls=%fused_computation.31 | convolution fusion | flops 1612709888 | bytes 8716800 | tf_op jit(solution)/shard_map/hbj,bjn,bjhp->bhnp/dot_general | solution.py:26
  35.5 21.8 %while.13 = (s32[]{:T(128)}, f32[16,128,64]{2,1,0:T(8,128)S(1)}, f32[8,16,128,64]{3,2,1,0:T(8,128)}, f32[8,16]{1,0:T(8,128)S(1)}, f32[8,16,128,64]{2,3,1,0:T(8,128)}, /*index=5*/s32[]{:T(128)}, s32[]{:T(128)}) while((s32[]{:T(128)}, f32[16,128,64]{2,1,0:T(8,128)S(1)}, f32[8,16,128,64]{3,2,1,0:T(8,128)}, f32[8,16]{1,0:T(8,128)S(1)}, ...), condition=%wide.region_2.3_spmd.clone, body=%wide.region_1.2_spmd.clone.sunk | while | flops 524291 | bytes 5243680 | solution.py:35
  35.5 1.0 bitcast_dynamic-update-slice_fusion.2
  36.5 1.1 constant_dynamic-slice_fusion.3
  37.6 0.3 copy.125
  38.2 1.1 bitcast_dynamic-update-slice_fusion.2
  39.3 1.1 constant_dynamic-slice_fusion.3
  40.4 0.3 copy.125
  40.9 1.1 bitcast_dynamic-update-slice_fusion.2
  42.0 1.1 constant_dynamic-slice_fusion.3
  43.7 1.1 bitcast_dynamic-update-slice_fusion.2
  44.7 1.1 constant_dynamic-slice_fusion.3
  46.4 1.0 bitcast_dynamic-update-slice_fusion.2
  47.4 1.1 constant_dynamic-slice_fusion.3
  49.1 1.1 bitcast_dynamic-update-slice_fusion.2
  50.2 1.1 constant_dynamic-slice_fusion.3
  51.2 0.3 copy.125
  51.8 1.1 bitcast_dynamic-update-slice_fusion.2
  52.9 1.1 constant_dynamic-slice_fusion.3
  54.5 1.1 bitcast_dynamic-update-slice_fusion.2
  55.6 1.1 constant_dynamic-slice_fusion.3
  57.3 0.9 copy.87
  58.2 0.7 all-gather.6.cloned.1.call-update
  59.0 0.7 all-gather.8.cloned.1.call-update
  59.8 0.6 dynamic-slice
  61.3 15.5 %all-reduce = f32[128]{0:T(128)S(1)} all-reduce(f32[128]{0:T(128)S(1)} %dynamic-update-slice), channel_id=2, replica_groups=mesh['ctx'=8,'exp'=4] {'ctx'}, use_global_device_ids=true, to_apply=%add | all-reduce | flops 128 | bytes 1024
  76.9 0.9 copy.78
  77.8 4.5 %reshape.93 = f32[8,128,16,64]{3,2,1,0:T(8,128)} reshape(bf16[1024,1024]{1,0:T(8,128)(2,1)S(1)} %copy-done.3) | data formatting | bytes 6291456 | tf_op jit(solution)/shard_map/reshape | solution.py:93
  82.3 7.2 %copy.94 = f32[8,128,16,64]{1,3,2,0:T(8,128)} copy(f32[8,128,16,64]{3,2,1,0:T(8,128)} %reshape.93) | data formatting | bytes 8388608 | tf_op jit(solution)/shard_map/reshape | solution.py:93
  89.6 2.5 mul.138
  92.0 5.4 %copy.90 = f32[1024,1024]{1,0:T(8,128)} copy(f32[1024,1024]{0,1:T(8,128)} %bitcast.98) | data formatting | bytes 8388608 | tf_op jit(solution)/shard_map/mul | solution.py:66
  98.0 12.5 %fusion.41 = f32[8,16,64,128]{3,2,1,0:T(8,128)} fusion(f32[8,16,128,64]{3,2,1,0:T(8,128)} %get-tuple-element.33, bf16[8,128,128,1]{2,1,3,0:T(8,128)(2,1)S(1)} %bitcast.95), kind=kOutput, calls=%fused_computation.70 | convolution fusion | flops 1610612736 | bytes 8650752 | tf_op jit(solution)/shard_map/bin,hbi,bhnp->bihp/dot_general | solution.py:38
  110.5 18.0 %fusion.2 = f32[8,16,64,128]{3,2,1,0:T(8,128)} fusion(f32[16,8,128]{2,0,1:T(8,128)S(1)} %copy_bitcast_fusion.2, f32[8,128,128]{2,1,0:T(8,128)S(1)} %fusion.40, f32[16,8,128]{2,0,1:T(8,128)S(1)} %copy.75, pred[128,128]{1,0:T(8,128)(4,1)S(1)} %iota_compare_fusion.3, f32[8,128,16,64]{1,3,2,0:T(8,128)S(1)} %copy-done.2, f32[8,16]{1,0:T(8,128)S(1)} %multiply_exponential_fusion), kind=kOutput, calls=%fused_computation.6 | convolution fusion | flops 1620049920 | bytes 9060864 | tf_op jit(solution)/shard_map/hbij,bjhp->bihp/dot_general | solution.py:24
  128.5 2.1 multiply_reduce_fusion
  130.6 9.6 %multiply_reduce_fusion.1 = (f32[8,128,16]{1,2,0:T(8,128)S(1)}, f32[8,128,16,64]{1,3,2,0:T(8,128)}) fusion(f32[8,128,16,64]{1,3,2,0:T(8,128)} %copy.94, f32[8,128,16,64]{1,3,2,0:T(8,128)} %copy.74, f32[16]{0:T(128)S(1)} %copy-done.10, f32[8,16]{1,0:T(8,128)S(1)} %multiply_exponential_fusion, bf16[8,128,128,1]{2,1,3,0:T(8,128)(2,1)S(1)} %bitcast.96, ...), kind=kOutput, calls=%fused_computation.20 | convolution fusion | flops 1625276416 | bytes 21955136 | tf_op jit(solution)/shard_map/bin,hbi,hnp->bihp/dot_general | solution.py:88
  140.2 7.2 %copy.110 = f32[8,128,16,64]{3,2,1,0:T(8,128)} copy(f32[8,128,16,64]{1,3,2,0:T(8,128)} %get-tuple-element.89) | data formatting | bytes 8388608 | tf_op jit(solution)/shard_map/reshape | solution.py:89
  147.4 7.7 %reshape.92 = f32[1024,1024]{1,0:T(8,128)} reshape(f32[8,128,16,64]{3,2,1,0:T(8,128)} %copy.110) | data formatting | bytes 8388608 | tf_op jit(solution)/shard_map/reshape | solution.py:89
  155.1 2.5 mul.149
  157.6 5.4 %copy.96 = f32[1024,1024]{1,0:T(8,128)} copy(f32[1024,1024]{0,1:T(8,128)} %bitcast.99) | data formatting | bytes 8388608 | tf_op jit(solution)/shard_map/mul | solution.py:97
  163.0 7.0 %multiply_convert_fusion = bf16[1024,1024]{1,0:T(8,128)(2,1)S(1)} fusion(f32[1024,1024]{1,0:T(8,128)} %copy.96, f32[1024,1024]{1,0:T(8,128)} %reshape.92, f32[1024,1024]{1,0:T(8,128)} %copy.90, f32[1024]{0:T(1024)S(1)} %copy-done.9, f32[1024]{0:T(1024)S(1)} %mul.134, bf16[1024,1024]{1,0:T(8,128)(2,1)S(1)} %copy-done.3, bf16[1024,1024]{1,0:T(8,128)(2,1)} %param.15), kind=kLoop, calls=%fused_computation.19 | loop fusion | flops 13631488 | bytes 18882560 | tf_op jit(solution)/shard_map/convert_element_type | solution.py:99
  170.0 1.3 copy-done.4
  171.3 0.7 convolution_convert_fusion.1
  172.0 1.7 collective-permute-start
  173.8 12.9 %collective-permute-done = bf16[256,1024]{1,0:T(8,128)(2,1)S(1)} collective-permute-done((bf16[256,1024]{1,0:T(8,128)(2,1)S(1)}, bf16[256,1024]{1,0:T(8,128)(2,1)S(1)}, u32[]{:S(2)}, u32[]{:S(2)}) %collective-permute-start) | collective-permute-done | bytes 524320 | tf_op jit(solution)/shard_map/ppermute | solution.py:106
  186.6 13.7 %collective-permute-done.1 = bf16[256,1024]{1,0:T(8,128)(2,1)S(1)} collective-permute-done((bf16[256,1024]{1,0:T(8,128)(2,1)S(1)}, bf16[256,1024]{1,0:T(8,128)(2,1)S(1)}, u32[]{:S(2)}, u32[]{:S(2)}) %collective-permute-start.1) | collective-permute-done | bytes 524320 | tf_op jit(solution)/shard_map/ppermute | solution.py:106
  200.3 12.8 %collective-permute-done.2 = bf16[256,1024]{1,0:T(8,128)(2,1)S(1)} collective-permute-done((bf16[256,1024]{1,0:T(8,128)(2,1)S(1)}, bf16[256,1024]{1,0:T(8,128)(2,1)S(1)}, u32[]{:S(2)}, u32[]{:S(2)}) %collective-permute-start.2) | collective-permute-done | bytes 524320 | tf_op jit(solution)/shard_map/ppermute | solution.py:106
  213.2 0.9 constant_dynamic-update-slice_fusion.7
  214.1 0.9 constant_dynamic-update-slice_fusion.6
  214.9 0.9 constant_dynamic-update-slice_fusion.5
  215.8 0.9 constant_dynamic-update-slice_fusion.4
  216.7 0.9 constant_dynamic-update-slice_fusion.3
  217.6 0.8 constant_dynamic-update-slice_fusion.2
  218.4 0.9 constant_dynamic-update-slice_fusion.1
  219.3 0.9 constant_dynamic-update-slice_fusion
  220.2 11.2 %convolution_convert_fusion = bf16[256,4096]{1,0:T(8,128)(2,1)} fusion(bf16[768,4096]{1,0:T(8,128)(2,1)} %all-gather.8.cloned.1.call-done, bf16[4096,768]{1,0:T(8,128)(2,1)} %all-gather.6.cloned.1.call-done, bf16[256,8192]{1,0:T(8,128)(2,1)} %constant_dynamic-update-slice_fusion, s32[]{:T(128)S(6)} %select_n.29), kind=kOutput, calls=%fused_computation.12 | convolution fusion | flops 3223257088 | bytes 16777220 | tf_op jit(solution)/shard_map/dot_general | solution.py:116
  231.5 44.6 %reduce-scatter.2.cloned.1.call-done = bf16[256,1024]{1,0:T(8,128)(2,1)} async-done(((bf16[256,4096]{1,0:T(8,128)(2,1)}), bf16[256,1024]{1,0:T(8,128)(2,1)}) %reduce-scatter.2.cloned.1.call-update) | async-done | bytes 524304 | tf_op jit(solution)/shard_map/reduce_scatter | solution.py:121
  276.0 3.3 %add_convert_fusion = bf16[1024,1024]{1,0:T(8,128)(2,1)} fusion(bf16[1024,1024]{1,0:T(8,128)(2,1)S(1)} %copy-done.5, bf16[256,1024]{1,0:T(8,128)(2,1)} %reduce-scatter.2.cloned.1.call-done, f32[1024]{0:T(1024)S(1)} %copy-done.12, s32[1024]{0:T(1024)S(1)} %copy-done.11), kind=kOutput, calls=%fused_computation.18 | convolution fusion | flops 541327360 | bytes 4726784 | tf_op jit(solution)/shard_map/dot_general | solution.py:125
  (87 shorter events, 5.5 us)
Async XLA Ops:
  6.5 91.2 %copy-start = (bf16[1024,128]{1,0:T(8,128)(2,1)S(1)}, bf16[1024,128]{1,0:T(8,128)(2,1)}, u32[]{:S(2)}) copy-start(bf16[1024,128]{1,0:T(8,128)(2,1)} %param.20) | copy-start | bytes 786436
  6.5 122.0 %all-gather.10.cloned.1.call-start = ((), (), s32[]{:S(2)}) async-start(), calls=%async_computation.4 | async-start | bytes 2359296 | tf_op jit(solution)/shard_map/all_gather | solution.py:78
  21.9 7.2 %copy-start.6 = (bf16[1024,128]{1,0:T(8,128)(2,1)S(1)}, bf16[1024,128]{1,0:T(8,128)(2,1)}, u32[]{:S(2)}) copy-start(bf16[1024,128]{1,0:T(8,128)(2,1)} %param.19) | copy-start | bytes 786436
  35.5 24.3 %copy-start.13 = (u32[32]{0:T(128)S(1)}, u32[32]{0:T(128)}, u32[]{:S(2)}) copy-start(u32[32]{0:T(128)} %constant.82) | copy-start | bytes 388
  57.3 20.5 %copy-start.3 = (bf16[1024,1024]{1,0:T(8,128)(2,1)S(1)}, bf16[1024,1024]{1,0:T(8,128)(2,1)}, u32[]{:S(2)}) copy-start(bf16[1024,1024]{1,0:T(8,128)(2,1)} %param.22) | copy-start | bytes 6291460
  58.2 162.0 %all-gather.6.cloned.1.call-start = ((), (), s32[]{:S(2)}) async-start(), calls=%async_computation.1 | async-start | bytes 7077888 | tf_op jit(solution)/shard_map/all_gather | solution.py:112
  59.0 161.2 %all-gather.8.cloned.1.call-start = ((), (), s32[]{:S(2)}) async-start(), calls=%async_computation.2 | async-start | bytes 7077888 | tf_op jit(solution)/shard_map/all_gather | solution.py:118
  59.7 216.3 %reduce-scatter.2.cloned.1.call-start = ((), (), s32[]{:S(2)}) async-start(), calls=%async_computation.3 | async-start | bytes 2621440 | tf_op jit(solution)/shard_map/reduce_scatter | solution.py:121
  92.0 5.4 %copy-start.10 = (f32[16]{0:T(128)S(1)}, f32[16]{0:T(128)}, u32[]{:S(2)}) copy-start(f32[16]{0:T(128)} %param.21) | copy-start | bytes 196
  92.0 5.7 %copy-start.8 = (f32[16,1024]{1,0:T(8,128)S(1)}, f32[16,1024]{1,0:T(8,128)}, u32[]{:S(2)}) copy-start(f32[16,1024]{1,0:T(8,128)} %param.17) | copy-start | bytes 196612
  92.0 5.7 %copy-start.7 = (bf16[1024,128]{1,0:T(8,128)(2,1)S(1)}, bf16[1024,128]{1,0:T(8,128)(2,1)}, u32[]{:S(2)}) copy-start(bf16[1024,128]{1,0:T(8,128)(2,1)} %param.19) | copy-start | bytes 786436
  98.0 12.5 %copy-start.2 = (f32[8,128,16,64]{1,3,2,0:T(8,128)S(1)}, f32[8,128,16,64]{1,3,2,0:T(8,128)}, u32[]{:S(2)}) copy-start(f32[8,128,16,64]{1,3,2,0:T(8,128)} %copy.74) | copy-start | bytes 12582916
  157.6 5.4 %copy-start.9 = (f32[1024]{0:T(1024)S(1)}, f32[1024]{0:T(1024)}, u32[]{:S(2)}) copy-start(f32[1024]{0:T(1024)} %param.23) | copy-start | bytes 12292
  163.0 8.3 %copy-start.11 = (s32[1024]{0:T(1024)S(1)}, s32[1024]{0:T(1024)}, u32[]{:S(2)}) copy-start(s32[1024]{0:T(1024)} %param.26) | copy-start | bytes 12292
  170.0 1.3 copy-start.4
  172.0 14.6 %collective-permute-start = (bf16[256,1024]{1,0:T(8,128)(2,1)S(1)}, bf16[256,1024]{1,0:T(8,128)(2,1)S(1)}, u32[]{:S(2)}, u32[]{:S(2)}) collective-permute-start(bf16[256,1024]{1,0:T(8,128)(2,1)S(1)} %convolution_convert_fusion.1), channel_id=1, source_target_pairs={{0,1},{1,2},{2,3},{3,0},{4,5},{5,6},{6,7},{7,4},{8,9},{9,10},{10,1... | collective-permute-start | bytes 1572872 | tf_op jit(solution)/shard_map/ppermute | solution.py:106
  186.6 13.7 %collective-permute-start.1 = (bf16[256,1024]{1,0:T(8,128)(2,1)S(1)}, bf16[256,1024]{1,0:T(8,128)(2,1)S(1)}, u32[]{:S(2)}, u32[]{:S(2)}) collective-permute-start(bf16[256,1024]{1,0:T(8,128)(2,1)S(1)} %collective-permute-done), channel_id=1, source_target_pairs={{0,1},{1,2},{2,3},{3,0},{4,5},{5,6},{6,7},{7,4},{8,9},{9,10},{10,1... | collective-permute-start | bytes 1572872 | tf_op jit(solution)/shard_map/ppermute | solution.py:106
  200.3 12.9 %collective-permute-start.2 = (bf16[256,1024]{1,0:T(8,128)(2,1)S(1)}, bf16[256,1024]{1,0:T(8,128)(2,1)S(1)}, u32[]{:S(2)}, u32[]{:S(2)}) collective-permute-start(bf16[256,1024]{1,0:T(8,128)(2,1)S(1)} %collective-permute-done.1), channel_id=1, source_target_pairs={{0,1},{1,2},{2,3},{3,0},{4,5},{5,6},{6,7},{7,4},{8,9},{9,10},{10,1... | collective-permute-start | bytes 1572872 | tf_op jit(solution)/shard_map/ppermute | solution.py:106
  220.2 55.9 %copy-start.5 = (bf16[1024,1024]{1,0:T(8,128)(2,1)S(1)}, bf16[1024,1024]{1,0:T(8,128)(2,1)}, u32[]{:S(2)}) copy-start(bf16[1024,1024]{1,0:T(8,128)(2,1)} %copy-done.4) | copy-start | bytes 6291460
  220.2 55.9 %copy-start.12 = (f32[1024]{0:T(1024)S(1)}, f32[1024]{0:T(1024)}, u32[]{:S(2)}) copy-start(f32[1024]{0:T(1024)} %param.27) | copy-start | bytes 12292
  220.2 59.1 %copy-start.1 = (bf16[1024,128]{1,0:T(8,128)(2,1)S(1)}, bf16[1024,128]{1,0:T(8,128)(2,1)}, u32[]{:S(2)}) copy-start(bf16[1024,128]{1,0:T(8,128)(2,1)} %param.20) | copy-start | bytes 786436
Sparse Core Ops, SparseCore 0:
  58.3 30.5 all-gather.9
  90.8 45.3 all-gather.5
  138.1 46.5 all-gather.7
  231.6 44.4 reduce-scatter.1
